TPU v7x, 512 devices: a whole 4x4x16 slice. The times are simulated.
512 devices in a mesh: row: 32 (over x, z_lo, core), col: 16 (over y, z_hi).
Axes of the slice: x: 4, y: 4, z: 16 (z_hi: 4, z_lo: 4; z = z_hi * 4 + z_lo), core: 2. Of those that a mesh axis runs over, the one named last changes fastest.
Arguments:
- features: bfloat16 [65536, 128], P(('row', 'col')), may hold values from -6 to 6
- weight: bfloat16 [128, 128], replicated, may hold values from -0.5 to 0.5
- adj_values: bfloat16 [32, 16, 16, 128, 128], P('row', 'col'), may hold values from -0.125 to 0.125
- tile_rows: int32 [32, 16, 16], P('row', 'col'), may hold values from 0 to 15
- tile_cols: int32 [32, 16, 16], P('row', 'col'), may hold values from 0 to 31
- cotangent: bfloat16 [65536, 128], P(('row', 'col')), may hold values from -6 to 6
Outputs:
- activations: float32 [65536, 128], P(('row', 'col'))
- grad_features: float32 [65536, 128], P(('row', 'col'))
- grad_weight: float32 [128, 128], replicated
All inputs are finite; a program needn't handle non-finite values.
Results may differ from a plain program's by a relative error of at most 0.0049.
Values may be sent and summed in bfloat16 or wider, within the bound.
No kernel may reach another device: no remote copies, remote signals or barrier semaphores. Data moves between devices by JAX's collectives and lax.ppermute only.
A program may use at most 64 MiB of HBM per device.

v0:
```python
import jax
import jax.numpy as jnp
from jax import lax
from jax.sharding import PartitionSpec as P


def per_device(features, weight, adj_values, tile_rows, tile_cols, cotangent):
    blocks = adj_values[0, 0]
    rows_id = tile_rows[0, 0]
    cols_id = tile_cols[0, 0]
    tile = blocks.shape[-1]
    owned = features.shape[0]
    width = features.shape[1]
    n_row = lax.axis_size("row")
    n_col = lax.axis_size("col")
    col_block = lax.all_gather(features, "row", axis=0, tiled=True)
    picked = col_block.reshape(-1, tile, width)[cols_id]
    prods = jnp.einsum("tab,tbf->taf", blocks, picked, preferred_element_type=jnp.float32)
    partial_rows = jax.ops.segment_sum(prods, rows_id, num_segments=n_col * owned // tile)
    aggregated = lax.psum_scatter(
        partial_rows.reshape(-1, width), "col", scatter_dimension=0, tiled=True
    )
    zed = aggregated.astype(jnp.bfloat16)
    pre = jnp.dot(zed, weight, preferred_element_type=jnp.float32)
    sig = jax.nn.sigmoid(pre)
    activations = pre * sig
    dpre = (cotangent.astype(jnp.float32) * sig * (1.0 + pre * (1.0 - sig))).astype(jnp.bfloat16)
    weight_part = lax.dot_general(
        zed, dpre, (((0,), (0,)), ((), ())), preferred_element_type=jnp.float32
    )
    grad_weight = lax.psum(weight_part, ("row", "col"))
    dzed = lax.dot_general(
        dpre, weight, (((1,), (1,)), ((), ())), preferred_element_type=jnp.float32
    ).astype(jnp.bfloat16)
    row_block = lax.all_gather(dzed, "col", axis=0, tiled=True)
    picked_back = row_block.reshape(-1, tile, width)[rows_id]
    prods_back = jnp.einsum("tab,taf->tbf", blocks, picked_back, preferred_element_type=jnp.float32)
    partial_cols = jax.ops.segment_sum(prods_back, cols_id, num_segments=n_row * owned // tile)
    grad_features = lax.psum_scatter(
        partial_cols.reshape(-1, width), "row", scatter_dimension=0, tiled=True
    )
    return (activations, grad_features, grad_weight)


def solution(mesh):
    return jax.shard_map(
        per_device,
        mesh=mesh,
        in_specs=(
            P(("row", "col"), None),
            P(),
            P("row", "col", None, None, None),
            P("row", "col", None),
            P("row", "col", None),
            P(("row", "col"), None),
        ),
        out_specs=(P(("row", "col"), None), P(("row", "col"), None), P()),
        check_vma=False,
    )
```

profile of v0, /device:TPU:16, one launch (start us, length us, event | category | flops | bytes accessed | tf_op | source)
XLA Modules:
  0.0 806.1 jit_solution(2386239688956795602)
XLA Ops:
  7.2 0.7 all-gather.2.cloned.1.call-update
  8.0 0.7 fusion.7
  8.6 69.6 %all-gather.2.cloned.1.call-done = bf16[4096,128]{1,0:T(8,128)(2,1)} async-done(((bf16[128,128]{1,0:T(8,128)(2,1)}), bf16[4096,128]{1,0:T(8,128)(2,1)}) %all-gather.2.cloned.1.call-update) | async-done | bytes 1048592 | tf_op jit(solution)/shard_map/all_gather | solution.py:16
  78.3 1.9 gather_fusion
  80.2 0.5 convolution_bitcast_fusion.1
  80.7 0.3 copy.12
  81.0 0.1 broadcast_in_dim.8
  81.1 0.2 copy-done.4
  81.3 1.6 scatter_fusion
  83.0 1.0 copy-done.2
  84.0 112.7 %reduce-scatter.3.cloned.1.call-done = f32[128,128]{1,0:T(8,128)} async-done(((f32[2048,128]{1,0:T(8,128)}), f32[128,128]{1,0:T(8,128)}) %reduce-scatter.3.cloned.1.call-update) | async-done | bytes 65552 | tf_op jit(solution)/shard_map/reduce_scatter | solution.py:20
  196.7 1.6 multiply_convert_fusion
  198.3 0.1 convolution_convert_fusion
  198.4 1.7 fusion.3
  200.2 52.1 %all_gather.7 = bf16[2048,128]{1,0:T(8,128)(2,1)S(1)} all-gather(bf16[128,128]{1,0:T(8,128)(2,1)S(1)} %convolution_convert_fusion), channel_id=1, replica_groups=mesh['row'=32,'col'=16] {'col'}, dimensions={0}, use_global_device_ids=true | all-gather | bytes 557056 | tf_op jit(solution)/shard_map/all_gather | solution.py:35
  252.3 0.6 gather_fusion.1
  252.9 0.4 convolution_bitcast_fusion
  253.3 1.3 copy.14
  254.6 0.2 broadcast_in_dim.9
  254.8 2.6 scatter_fusion.1
  257.5 1.3 copy-done.1
  258.8 389.8 %all-reduce.2.cloned.1.call-done = f32[128,128]{1,0:T(8,128)} async-done(((f32[128,128]{1,0:T(8,128)}), f32[128,128]{1,0:T(8,128)}) %all-reduce.2.cloned.1.call-update) | async-done | bytes 65552 | tf_op jit(solution)/shard_map/psum | solution.py:31
  648.6 149.5 %reduce-scatter.5.cloned.1.call-done = f32[128,128]{1,0:T(8,128)} async-done(((f32[4096,128]{1,0:T(8,128)}), f32[128,128]{1,0:T(8,128)}) %reduce-scatter.5.cloned.1.call-update) | async-done | bytes 65552 | tf_op jit(solution)/shard_map/reduce_scatter | solution.py:39
  798.1 1.5 copy.20
  (21 shorter events, 0.3 us)
Async XLA Ops:
  7.2 73.0 %copy-start = (bf16[1,1,16,128,128]{4,3,2,1,0:T(8,128)(2,1)S(1)}, bf16[1,1,16,128,128]{4,3,2,1,0:T(8,128)(2,1)}, u32[]{:S(2)}) copy-start(bf16[1,1,16,128,128]{4,3,2,1,0:T(8,128)(2,1)} %param.8) | copy-start | bytes 1572868
  7.2 71.1 %all-gather.2.cloned.1.call-start = ((), (), s32[]{:S(2)}) async-start(), calls=%async_computation.2 | async-start | bytes 1081344 | tf_op jit(solution)/shard_map/all_gather | solution.py:16
  7.9 188.8 %reduce-scatter.3.cloned.1.call-start = ((), (), s32[]{:S(2)}) async-start(), calls=%async_computation.3 | async-start | bytes 1114112 | tf_op jit(solution)/shard_map/reduce_scatter | solution.py:20
  80.7 0.7 copy-start.4
  81.3 115.3 %copy-start.3 = (bf16[128,128]{1,0:T(8,128)(2,1)S(1)}, bf16[128,128]{1,0:T(8,128)(2,1)}, u32[]{:S(2)}) copy-start(bf16[128,128]{1,0:T(8,128)(2,1)} %param.7) | copy-start | bytes 98308
  81.3 115.3 %copy-start.6 = (bf16[128,128]{1,0:T(8,128)(2,1)S(1)}, bf16[128,128]{1,0:T(8,128)(2,1)}, u32[]{:S(2)}) copy-start(bf16[128,128]{1,0:T(8,128)(2,1)} %param.11) | copy-start | bytes 98308
  82.9 1.0 copy-start.2
  83.9 564.6 %all-reduce.2.cloned.1.call-start = ((), (), s32[]{:S(2)}) async-start(), calls=%async_computation.5 | async-start | bytes 131072 | tf_op jit(solution)/shard_map/psum | solution.py:31
  200.2 597.9 %reduce-scatter.5.cloned.1.call-start = ((), (), s32[]{:S(2)}) async-start(), calls=%async_computation.4 | async-start | bytes 2162688 | tf_op jit(solution)/shard_map/reduce_scatter | solution.py:39
  253.3 1.6 copy-start.5
  257.4 1.3 copy-start.1
Sparse Core Ops, SparseCore 0:
  10.1 68.0 all-gather.1
  84.1 112.5 reduce-scatter.2
  202.7 445.8 all-reduce.1
  651.8 146.2 reduce-scatter.4
where the time goes:
time: 806 us
  waiting for transfers between devices  722 us (90%)
  blocking collectives  52.1 us (6%)
  between operations  13.9 us (2%)
  local copies, waits for them, and re-layouts  8.49 us (1%)
    psum x1, waiting for transfers between devices, per_device(): grad_weight = lax.psum(weight_part, ('row', 'col'))  390 us
    reduce_scatter x1, waiting for transfers between devices, per_device(): lax.psum_scatter(partial_cols.reshape(-1, width), 'row', scatter_dimensio...  150 us
    reduce_scatter x1, waiting for transfers between devices, per_device(): lax.psum_scatter(partial_rows.reshape(-1, width), 'col', scatter_dimensio...  113 us
    all_gather x1, waiting for transfers between devices, per_device(): col_block = lax.all_gather(features, 'row', axis=0, tiled=True)  69.6 us
    all_gather x1, blocking collectives, per_device(): row_block = lax.all_gather(dzed, 'col', axis=0, tiled=True)  52.1 us
  transfers between devices with their start and end apart: 4, of which 4 were waited for; matrix products, arithmetic and copies ran while one was open for 1% of the time, Pallas kernels for 0%

commit v1 on v0

--- a/solution.py
+++ b/solution.py
@@ -13,7 +13,9 @@
     width = features.shape[1]
     n_row = lax.axis_size("row")
     n_col = lax.axis_size("col")
-    col_block = lax.all_gather(features, "row", axis=0, tiled=True)
+    col_block = jnp.concatenate(
+        lax.all_to_all(jnp.stack([features] * lax.axis_size("row")), "row", 0, 0), axis=0
+    )
     picked = col_block.reshape(-1, tile, width)[cols_id]
     prods = jnp.einsum("tab,tbf->taf", blocks, picked, preferred_element_type=jnp.float32)
     partial_rows = jax.ops.segment_sum(prods, rows_id, num_segments=n_col * owned // tile)

time: 806 us -> 775 us (0.962)
  the two profiles are of different devices: /device:TPU:16 before, /device:TPU:8 now
where the time goes in v1:
time: 775 us; the launch traced here: 774 us
  waiting for transfers between devices  680 us (88%)
  blocking collectives  53.8 us (7%)
  between operations  13.9 us (2%)
  local copies, waits for them, and re-layouts  9.25 us (1%)
  starting transfers between devices  8.87 us (1%)
    psum x1, waiting for transfers between devices, per_device(): grad_weight = lax.psum(weight_part, ('row', 'col'))  388 us
    reduce_scatter x1, waiting for transfers between devices, per_device(): lax.psum_scatter(partial_cols.reshape(-1, width), 'row', scatter_dimensio...  149 us
    reduce_scatter x1, waiting for transfers between devices, per_device(): lax.psum_scatter(partial_rows.reshape(-1, width), 'col', scatter_dimensio...  114 us
    all_gather x1, blocking collectives, per_device(): row_block = lax.all_gather(dzed, 'col', axis=0, tiled=True)  53.8 us
    all_to_all x1, waiting for transfers between devices, per_device(): lax.all_to_all(jnp.stack([features] * lax.axis_size('row')), 'row', 0, 0)  27.8 us
  transfers between devices with their start and end apart: 4, of which 4 were waited for; matrix products, arithmetic and copies ran while one was open for 1% of the time, Pallas kernels for 0%

profile of v1, /device:TPU:8, one launch (start us, length us, event | category | flops | bytes accessed | tf_op | source)
XLA Modules:
  0.0 774.2 jit_solution(240425382897491113)
XLA Ops:
  7.2 2.0 stack.2
  9.2 8.8 %all-to-all-start = ((bf16[32,128,128]{2,1,0:T(8,128)(2,1)}), bf16[32,128,128]{2,1,0:T(8,128)(2,1)S(1)}, u32[]{:S(2)}, u32[]{:S(2)}) async-start(bf16[32,128,128]{2,1,0:T(8,128)(2,1)} %stack.2), calls=%async_computation | async-start | bytes 2097152 | tf_op jit(solution)/shard_map/all_to_all | solution.py:17
  18.1 27.8 %all-to-all-done = bf16[32,128,128]{2,1,0:T(8,128)(2,1)S(1)} async-done(((bf16[32,128,128]{2,1,0:T(8,128)(2,1)}), bf16[32,128,128]{2,1,0:T(8,128)(2,1)S(1)}, u32[]{:S(2)}, u32[]{:S(2)}) %all-to-all-start) | async-done | bytes 1048608 | tf_op jit(solution)/shard_map/all_to_all | solution.py:17
  45.8 0.6 gather_fusion
  46.5 0.5 convolution_bitcast_fusion.1
  47.0 0.3 copy.12
  47.3 0.1 broadcast_in_dim.8
  47.4 0.2 copy-done.4
  47.7 1.6 scatter_fusion
  49.3 1.0 copy-done.2
  50.3 114.2 %reduce-scatter.3.cloned.1.call-done = f32[128,128]{1,0:T(8,128)} async-done(((f32[2048,128]{1,0:T(8,128)}), f32[128,128]{1,0:T(8,128)}) %reduce-scatter.3.cloned.1.call-update) | async-done | bytes 65552 | tf_op jit(solution)/shard_map/reduce_scatter | solution.py:22
  164.5 1.6 multiply_convert_fusion
  166.2 0.1 convolution_convert_fusion
  166.3 1.7 fusion.3
  168.1 53.8 %all_gather.3 = bf16[2048,128]{1,0:T(8,128)(2,1)S(1)} all-gather(bf16[128,128]{1,0:T(8,128)(2,1)S(1)} %convolution_convert_fusion), channel_id=1, replica_groups=mesh['row'=32,'col'=16] {'col'}, dimensions={0}, use_global_device_ids=true | all-gather | bytes 557056 | tf_op jit(solution)/shard_map/all_gather | solution.py:37
  221.8 0.6 gather_fusion.1
  222.5 0.4 convolution_bitcast_fusion
  222.9 1.3 copy.14
  224.2 0.2 broadcast_in_dim.9
  224.4 2.6 scatter_fusion.1
  227.0 1.3 copy-done.1
  228.4 388.4 %all-reduce.2.cloned.1.call-done = f32[128,128]{1,0:T(8,128)} async-done(((f32[128,128]{1,0:T(8,128)}), f32[128,128]{1,0:T(8,128)}) %all-reduce.2.cloned.1.call-update) | async-done | bytes 65552 | tf_op jit(solution)/shard_map/psum | solution.py:33
  616.8 149.4 %reduce-scatter.5.cloned.1.call-done = f32[128,128]{1,0:T(8,128)} async-done(((f32[4096,128]{1,0:T(8,128)}), f32[128,128]{1,0:T(8,128)}) %reduce-scatter.5.cloned.1.call-update) | async-done | bytes 65552 | tf_op jit(solution)/shard_map/reduce_scatter | solution.py:41
  766.2 1.5 copy.20
  (21 shorter events, 0.2 us)
Async XLA Ops:
  7.2 39.3 %copy-start = (bf16[1,1,16,128,128]{4,3,2,1,0:T(8,128)(2,1)S(1)}, bf16[1,1,16,128,128]{4,3,2,1,0:T(8,128)(2,1)}, u32[]{:S(2)}) copy-start(bf16[1,1,16,128,128]{4,3,2,1,0:T(8,128)(2,1)} %param.8) | copy-start | bytes 1572868
  7.2 10.8 %copy-start.5 = (s32[1,1,16]{2,1,0:T(1,128)S(1)}, s32[1,1,16]{2,1,0:T(1,128)}, u32[]{:S(2)}) copy-start(s32[1,1,16]{2,1,0:T(1,128)} %param.10) | copy-start | bytes 196
  9.2 36.6 %all-to-all-start = ((bf16[32,128,128]{2,1,0:T(8,128)(2,1)}), bf16[32,128,128]{2,1,0:T(8,128)(2,1)S(1)}, u32[]{:S(2)}, u32[]{:S(2)}) async-start(bf16[32,128,128]{2,1,0:T(8,128)(2,1)} %stack.2), calls=%async_computation | async-start | bytes 2097152 | tf_op jit(solution)/shard_map/all_to_all | solution.py:17
  18.0 146.6 %reduce-scatter.3.cloned.1.call-start = ((), (), s32[]{:S(2)}) async-start(), calls=%async_computation.3 | async-start | bytes 1114112 | tf_op jit(solution)/shard_map/reduce_scatter | solution.py:22
  47.0 0.7 copy-start.4
  47.6 116.9 %copy-start.3 = (bf16[128,128]{1,0:T(8,128)(2,1)S(1)}, bf16[128,128]{1,0:T(8,128)(2,1)}, u32[]{:S(2)}) copy-start(bf16[128,128]{1,0:T(8,128)(2,1)} %param.7) | copy-start | bytes 98308
  47.6 116.9 %copy-start.6 = (bf16[128,128]{1,0:T(8,128)(2,1)S(1)}, bf16[128,128]{1,0:T(8,128)(2,1)}, u32[]{:S(2)}) copy-start(bf16[128,128]{1,0:T(8,128)(2,1)} %param.11) | copy-start | bytes 98308
  49.3 1.0 copy-start.2
  50.2 566.5 %all-reduce.2.cloned.1.call-start = ((), (), s32[]{:S(2)}) async-start(), calls=%async_computation.5 | async-start | bytes 131072 | tf_op jit(solution)/shard_map/psum | solution.py:33
  168.0 598.2 %reduce-scatter.5.cloned.1.call-start = ((), (), s32[]{:S(2)}) async-start(), calls=%async_computation.4 | async-start | bytes 2162688 | tf_op jit(solution)/shard_map/reduce_scatter | solution.py:41
  227.0 1.3 copy-start.1
Sparse Core Ops, SparseCore 0:
  50.4 114.1 reduce-scatter.2
  170.5 446.1 all-reduce.1
  620.1 145.9 reduce-scatter.4
